TPU v7x, 32 devices: a whole 2x2x4 slice. The times are simulated.
32 devices in a mesh: row: 4 (over y, core), col: 8 (over z, x).
Axes of the slice: x: 2, y: 2, z: 4, core: 2. Of those that a mesh axis runs over, the one named last changes fastest.
Arguments:
- rhs_tile: float32 [18432, 9216], P('row', 'col'), may hold values from -6 to 6
- factor: float32 [18432, 1536], P('row', 'col'), may hold values from -1 to 2.5, as said below
Outputs:
- whitened: float32 [18432, 9216], P('row', 'col')
Inputs may be any that keep to these rules, and one draw needn't show every extreme that they name: In elimination order factor is lower triangular: entries above the diagonal are zero, diagonal entries are at least 0.7.
All inputs are finite; a program needn't handle non-finite values.
Results may differ from a plain program's by a relative error of at most 0.0001.
Values sent between devices are 32-bit elements; how exact they have to be, the bound alone decides.
A program may use at most 128 MiB of HBM per device.

v0:
```python
import jax
import jax.numpy as jnp
from jax import lax
from jax.sharding import PartitionSpec as P

PANEL = 512
PANELS = 3


def local(rhs_tile, factor):
    row_count = lax.axis_size("row")
    col_count = lax.axis_size("col")
    row_piece = PANEL // row_count
    col_piece = PANEL // col_count
    my_row = lax.axis_index("row")
    result = rhs_tile
    for panel_index in range(PANELS):
        start_row = panel_index * row_piece
        end_row = start_row + row_piece
        first_col = panel_index * col_piece
        strip = lax.all_gather(
            factor[start_row:end_row, first_col : first_col + col_piece], "col", axis=1, tiled=True
        )
        diagonal = lax.all_gather(strip, "row", axis=0, tiled=True)
        own_rows = result[start_row:end_row]
        stacked = lax.all_gather(own_rows, "row", axis=0, tiled=True)
        solved = jax.scipy.linalg.solve_triangular(diagonal, stacked, lower=True)
        mine_rows = lax.dynamic_slice_in_dim(solved, my_row * row_piece, row_piece, 0)
        trailing = result[end_row:]

        def add_panel(total, piece, start, solved=solved):
            return jnp.dot(
                piece, solved, precision=lax.Precision.HIGHEST, preferred_element_type=jnp.float32
            )

        initial = jnp.zeros(trailing.shape, jnp.float32)
        update = add_panel(
            initial,
            lax.all_gather(
                factor[end_row:, first_col : first_col + col_piece], "col", axis=1, tiled=True
            ),
            jnp.int32(0),
        )
        result = jnp.concatenate([result[:start_row], mine_rows, trailing - update], axis=0)
    return result


def solution(mesh):
    in_specs = (P("row", "col"), P("row", "col"))
    out_specs = P("row", "col")
    return jax.shard_map(local, mesh=mesh, in_specs=in_specs, out_specs=out_specs, check_vma=False)
```

profile of v0, /device:TPU:0, one launch (start us, length us, event | category | flops | bytes accessed | tf_op | source)
XLA Modules:
  0.0 708.7 jit_solution(17606545993645377573)
XLA Ops:
  7.3 34.5 %all_gather.36 = f32[128,512]{0,1:T(8,128)} all-gather(f32[128,64]{0,1:T(8,128)S(1)} %get-tuple-element.73), channel_id=1, replica_groups=mesh['row'=4,'col'=8] {'col'}, dimensions={1}, use_global_device_ids=true | all-gather | bytes 294912 | tf_op jit(solution)/shard_map/all_gather | solution.py:21
  46.4 32.8 %all_gather.39 = f32[128,512]{0,1:T(8,128)} all-gather(f32[128,64]{0,1:T(8,128)S(1)} %get-tuple-element.72), channel_id=1, replica_groups=mesh['row'=4,'col'=8] {'col'}, dimensions={1}, use_global_device_ids=true | all-gather | bytes 294912 | tf_op jit(solution)/shard_map/all_gather | solution.py:21
  79.2 15.6 %slice.61 = f32[4480,1152]{1,0:T(8,128)} slice(f32[4608,1152]{1,0:T(8,128)} %param.4), slice={[128:4608], [0:1152]} | slice | bytes 41287680 | tf_op jit(solution)/shard_map/slice | solution.py:29
  94.8 22.6 %copy.36 = f32[4480,1152]{0,1:T(8,128)} copy(f32[4480,1152]{1,0:T(8,128)} %slice.61) | data formatting | bytes 41287680
  118.9 8.5 %while.6 = (s32[]{:T(128)}, f32[512,512]{0,1:T(8,128)S(1)}, s32[4,2]{0,1:T(2,128)S(1)}, f32[4,128,128]{2,1,0:T(8,128)S(1)}, s32[]{:T(128)}) while((s32[]{:T(128)}, f32[512,512]{0,1:T(8,128)S(1)}, s32[4,2]{0,1:T(2,128)S(1)}, f32[4,128,128]{2,1,0:T(8,128)S(1)}, s32[]{:T(128)}) %tuple.54), condition=%wide.while_cond, body=%wide.while_body.sunk | while | flops 2 | bytes 393321 | solution.py:27
  127.4 39.3 %custom-call.5 = f32[4,128,128]{1,2,0:T(8,128)S(1)} custom-call(f32[4,128,128]{2,1,0:T(8,128)S(1)} %get-tuple-element.26), custom_call_target="InvertDiagBlocksLowerTriangular" | custom-call | tf_op jit(solution)/shard_map/jit(_solve_triangular)/triangular_solve | solution.py:27
  175.6 46.5 %all-gather.16.cloned.1.call-done = f32[4480,512]{0,1:T(8,128)} async-done(((f32[4480,64]{0,1:T(8,128)}), f32[4480,512]{0,1:T(8,128)}) %all-gather.16.cloned.1.call-update) | async-done | bytes 9175056 | tf_op jit(solution)/shard_map/all_gather | solution.py:39
  222.1 41.0 %fusion = f32[4480,1152]{0,1:T(8,128)S(1)} fusion(f32[4480,1152]{0,1:T(8,128)} %copy.36, f32[4480,512]{0,1:T(8,128)} %all-gather.16.cloned.1.call-done, f32[128,1152]{1,0:T(8,128)S(1)} %fusion.50, f32[128,1152]{1,0:T(8,128)S(1)} %fusion.51, f32[128,1152]{1,0:T(8,128)S(1)} %fusion.53, f32[128,1152]{1,0:T(8,128)S(1)} %fusion.34), kind=kOutput, calls=%fused_computation.9 | convolution fusion | flops 31715868672 | bytes 52822016 | tf_op jit(solution)/shard_map/dot_general | solution.py:32
  263.1 7.4 %copy-done = f32[4480,1152]{0,1:T(8,128)} copy-done((f32[4480,1152]{0,1:T(8,128)}, f32[4480,1152]{0,1:T(8,128)S(1)}, u32[]{:S(2)}) %copy-start) | copy-done | bytes 20643864
  274.0 32.8 %all_gather.43 = f32[128,512]{0,1:T(8,128)} all-gather(f32[128,64]{0,1:T(8,128)S(1)} %get-tuple-element.71), channel_id=1, replica_groups=mesh['row'=4,'col'=8] {'col'}, dimensions={1}, use_global_device_ids=true | all-gather | bytes 294912 | tf_op jit(solution)/shard_map/all_gather | solution.py:21
  309.2 12.3 %while.7 = (s32[]{:T(128)}, f32[512,512]{0,1:T(8,128)}, s32[4,2]{0,1:T(2,128)S(1)}, f32[4,128,128]{2,1,0:T(8,128)S(1)}, s32[]{:T(128)}) while((s32[]{:T(128)}, f32[512,512]{0,1:T(8,128)}, s32[4,2]{0,1:T(2,128)S(1)}, f32[4,128,128]{2,1,0:T(8,128)S(1)}, s32[]{:T(128)}) %tuple.81), condition=%wide.while_cond.clone, body=%wide.while_body.clone.sunk | while | flops 2 | bytes 393321 | solution.py:27
  321.5 39.3 %custom-call.6 = f32[4,128,128]{1,2,0:T(8,128)S(1)} custom-call(f32[4,128,128]{2,1,0:T(8,128)S(1)} %get-tuple-element.27), custom_call_target="InvertDiagBlocksLowerTriangular" | custom-call | tf_op jit(solution)/shard_map/jit(_solve_triangular)/triangular_solve | solution.py:27
  367.8 3.2 convolution_subtract_fusion.5
  373.6 4.3 convolution_subtract_fusion.1
  379.3 47.6 %all-gather.22.cloned.1.call-done = f32[4352,512]{0,1:T(8,128)} async-done(((f32[4352,64]{0,1:T(8,128)}), f32[4352,512]{0,1:T(8,128)}) %all-gather.22.cloned.1.call-update) | async-done | bytes 8912912 | tf_op jit(solution)/shard_map/all_gather | solution.py:39
  426.9 41.9 %fusion.2 = f32[4352,1152]{0,1:T(8,128)} fusion(f32[4352,512]{0,1:T(8,128)} %all-gather.22.cloned.1.call-done, f32[4480,1152]{0,1:T(8,128)} %copy-done, f32[128,1152]{0,1:T(8,128)S(1)} %fusion.46, f32[128,1152]{0,1:T(8,128)} %copy.22, f32[128,1152]{0,1:T(8,128)} %copy.21, f32[128,1152]{0,1:T(8,128)} %copy.20), kind=kOutput, calls=%fused_computation.11 | convolution fusion | flops 30809751552 | bytes 51380224 | tf_op jit(solution)/shard_map/dot_general | solution.py:32
  475.5 12.0 %while.8 = (s32[]{:T(128)}, f32[512,512]{0,1:T(8,128)}, s32[4,2]{0,1:T(2,128)S(1)}, f32[4,128,128]{2,1,0:T(8,128)S(1)}, s32[]{:T(128)}) while((s32[]{:T(128)}, f32[512,512]{0,1:T(8,128)}, s32[4,2]{0,1:T(2,128)S(1)}, f32[4,128,128]{2,1,0:T(8,128)S(1)}, s32[]{:T(128)}) %tuple.82), condition=%wide.while_cond.clone.1, body=%wide.while_body.clone.1.sunk | while | flops 2 | bytes 393321 | solution.py:27
  487.5 40.1 %custom-call.7 = f32[4,128,128]{1,2,0:T(8,128)} custom-call(f32[4,128,128]{2,1,0:T(8,128)S(1)} %get-tuple-element.28), custom_call_target="InvertDiagBlocksLowerTriangular" | custom-call | tf_op jit(solution)/shard_map/jit(_solve_triangular)/triangular_solve | solution.py:27
  535.8 3.2 convolution_subtract_fusion.3
  540.7 4.3 convolution_subtract_fusion
  547.6 75.9 %all-gather.26.cloned.1.call-done = f32[4224,512]{0,1:T(8,128)} async-done(((f32[4224,64]{0,1:T(8,128)}), f32[4224,512]{0,1:T(8,128)}) %all-gather.26.cloned.1.call-update) | async-done | bytes 8650768 | tf_op jit(solution)/shard_map/all_gather | solution.py:39
  623.5 41.2 %fusion.1 = f32[4224,1152]{0,1:T(8,128)} fusion(f32[4224,512]{0,1:T(8,128)} %all-gather.26.cloned.1.call-done, f32[4352,1152]{0,1:T(8,128)} %fusion.2, f32[128,1152]{0,1:T(8,128)S(1)} %fusion.42, f32[128,1152]{0,1:T(8,128)S(1)} %copy.27, f32[128,1152]{0,1:T(8,128)S(1)} %copy.26, f32[128,1152]{0,1:T(8,128)S(1)} %copy.25), kind=kOutput, calls=%fused_computation.10 | convolution fusion | flops 29903634432 | bytes 49938432 | tf_op jit(solution)/shard_map/dot_general | solution.py:32
  664.7 15.0 %pad_maximum_fusion = f32[4608,1152]{0,1:T(8,128)} fusion(f32[4224,1152]{0,1:T(8,128)} %fusion.1, f32[128,1152]{0,1:T(8,128)S(1)} %copy-done.10, f32[128,1152]{0,1:T(8,128)S(1)} %copy-done.9, f32[128,1152]{0,1:T(8,128)S(1)} %copy-done.8), kind=kLoop, calls=%fused_computation.12 | loop fusion | flops 15925248 | bytes 42467328 | tf_op jit(solution)/shard_map/concatenate | solution.py:44
  679.7 22.1 %copy.30 = f32[4608,1152]{1,0:T(8,128)} copy(f32[4608,1152]{0,1:T(8,128)} %pad_maximum_fusion) | data formatting | bytes 42467328 | tf_op jit(solution)/shard_map/concatenate | solution.py:44
  (154 shorter events, 83.3 us)
Async XLA Ops:
  6.5 110.9 %all-gather.10.cloned.1.call-start = ((), (), s32[]{:S(2)}) async-start(), calls=%async_computation | async-start | bytes 1310720 | tf_op jit(solution)/shard_map/all_gather | solution.py:24
  41.9 124.9 %all-gather.12.cloned.1.call-start = ((), (), s32[]{:S(2)}) async-start(), calls=%async_computation.1 | async-start | bytes 2949120 | tf_op jit(solution)/shard_map/all_gather | solution.py:26
  43.9 178.2 %all-gather.16.cloned.1.call-start = ((), (), s32[]{:S(2)}) async-start(), calls=%async_computation.3 | async-start | bytes 10321920 | tf_op jit(solution)/shard_map/all_gather | solution.py:39
  46.3 260.5 %all-gather.14.cloned.1.call-start = ((), (), s32[]{:S(2)}) async-start(), calls=%async_computation.2 | async-start | bytes 1310720 | tf_op jit(solution)/shard_map/all_gather | solution.py:24
  79.2 281.7 %all-gather.18.cloned.1.call-start = ((), (), s32[]{:S(2)}) async-start(), calls=%async_computation.4 | async-start | bytes 2949120 | tf_op jit(solution)/shard_map/all_gather | solution.py:26
  127.4 43.7 %copy-start.6 = (f32[512,512]{0,1:T(8,128)}, f32[512,512]{0,1:T(8,128)S(1)}, u32[]{:S(2)}) copy-start(f32[512,512]{0,1:T(8,128)S(1)} %get-tuple-element.226) | copy-start | bytes 3145732
  166.8 4.3 copy-start.7
  175.6 87.6 %copy-start.1 = (f32[128,1152]{1,0:T(8,128)}, f32[128,1152]{1,0:T(8,128)S(1)}, u32[]{:S(2)}) copy-start(f32[128,1152]{1,0:T(8,128)S(1)} %fusion.50) | copy-start | bytes 1769476
  263.1 7.4 %copy-start = (f32[4480,1152]{0,1:T(8,128)}, f32[4480,1152]{0,1:T(8,128)S(1)}, u32[]{:S(2)}) copy-start(f32[4480,1152]{0,1:T(8,128)S(1)} %fusion) | copy-start | bytes 61931524
  271.5 155.4 %all-gather.22.cloned.1.call-start = ((), (), s32[]{:S(2)}) async-start(), calls=%async_computation.6 | async-start | bytes 10027008 | tf_op jit(solution)/shard_map/all_gather | solution.py:39
  273.9 199.2 %all-gather.20.cloned.1.call-start = ((), (), s32[]{:S(2)}) async-start(), calls=%async_computation.5 | async-start | bytes 1310720 | tf_op jit(solution)/shard_map/all_gather | solution.py:24
  306.8 223.8 %all-gather.24.cloned.1.call-start = ((), (), s32[]{:S(2)}) async-start(), calls=%async_computation.7 | async-start | bytes 2949120 | tf_op jit(solution)/shard_map/all_gather | solution.py:26
  360.8 5.9 copy-start.12
  470.7 152.7 %all-gather.26.cloned.1.call-start = ((), (), s32[]{:S(2)}) async-start(), calls=%async_computation.8 | async-start | bytes 9732096 | tf_op jit(solution)/shard_map/all_gather | solution.py:39
  473.1 54.6 %copy-start.2 = (f32[128,1152]{1,0:T(8,128)S(1)}, f32[128,1152]{1,0:T(8,128)}, u32[]{:S(2)}) copy-start(f32[128,1152]{1,0:T(8,128)} %copy-done.1) | copy-start | bytes 1769476
  527.9 1.2 copy-start.3
  527.9 1.3 copy-start.4
  527.9 1.6 copy-start.5
  529.5 1.1 copy-start.11
  547.6 117.1 %copy-start.8 = (f32[128,1152]{0,1:T(8,128)S(1)}, f32[128,1152]{0,1:T(8,128)}, u32[]{:S(2)}) copy-start(f32[128,1152]{0,1:T(8,128)} %copy.29) | copy-start | bytes 1769476
  547.6 117.1 %copy-start.9 = (f32[128,1152]{0,1:T(8,128)S(1)}, f32[128,1152]{0,1:T(8,128)}, u32[]{:S(2)}) copy-start(f32[128,1152]{0,1:T(8,128)} %constant_dynamic-slice_fusion.4) | copy-start | bytes 1769476
  623.5 41.2 %copy-start.10 = (f32[128,1152]{0,1:T(8,128)S(1)}, f32[128,1152]{0,1:T(8,128)}, u32[]{:S(2)}) copy-start(f32[128,1152]{0,1:T(8,128)} %constant_dynamic-slice_fusion.3) | copy-start | bytes 1769476
Sparse Core Ops, SparseCore 0:
  42.0 17.7 all-gather.9
  61.3 24.0 all-gather.11
  87.6 134.4 all-gather.15
  223.5 14.9 all-gather.13
  271.6 22.4 all-gather.17
  296.1 130.7 all-gather.21
  428.5 15.0 all-gather.19
  470.8 22.7 all-gather.23
  495.8 127.5 all-gather.25
where the time goes:
time: 718 us; the launch traced here: 709 us
  waiting for transfers between devices  170 us (24%)
  matrix products  163 us (23%)
  other arithmetic  140 us (19%)
  local copies, waits for them, and re-layouts  120 us (17%)
  blocking collectives  100 us (14%)
  between operations  14.1 us (2%)
    all_gather x3, waiting for transfers between devices, local(): lax.all_gather(factor[end_row:, first_col:first_col + col_piece], 'col',...  170 us
    another operation x10, other arithmetic, local(): solved = jax.scipy.linalg.solve_triangular(diagonal, stacked, lower=True)  125 us
    dot_general x3, matrix products, add_panel(): jnp.dot(piece, solved, precision=lax.Precision.HIGHEST, preferred_element...  124 us
    all_gather x3, blocking collectives, local(): lax.all_gather(factor[start_row:end_row, first_col:first_col + col_piece]...  100 us
    another operation x21, matrix products, local(): solved = jax.scipy.linalg.solve_triangular(diagonal, stacked, lower=True)  39.1 us
    another operation x70, local copies, waits for them, and re-layouts, local(): solved = jax.scipy.linalg.solve_triangular(diagonal, stacked, lower=True)  36 us
    unnamed x27, local copies, waits for them, and re-layouts  30.6 us
    concatenate x1, local copies, waits for them, and re-layouts, local(): jnp.concatenate([result[:start_row], mine_rows, trailing - update], axis=0)  22.1 us
  transfers between devices with their start and end apart: 9, of which 3 were waited for; matrix products, arithmetic and copies ran while one was open for 47% of the time, Pallas kernels for 0%

commit v1 on v0

v1 whole, which is shorter than its diff:
```python
import functools
import math

import jax
import jax.numpy as jnp
from jax import lax
from jax.experimental import pallas as pl
from jax.experimental.pallas import tpu as pltpu
from jax.sharding import PartitionSpec as P

PANEL = 512
PANELS = 3
HIGHEST = lax.Precision.HIGHEST
MESH = pl.DeviceIdType.MESH


def gather_kernel(outer, inner, tiles, first, rows, own_ref, full_ref, send_sem, recv_sem, local_sem):
    row = lax.axis_index("row")
    col = lax.axis_index("col")
    a, b = lax.div(col, inner), lax.rem(col, inner)
    sides = ((1, 0), (-1, 0), (0, 1), (0, -1))

    def inside(da, db):
        return (a + da >= 0) & (a + da < outer) & (b + db >= 0) & (b + db < inner)

    def place(da, db):
        return (a + da) * inner + b + db

    barrier = pltpu.get_barrier_semaphore()
    for da, db in sides:

        @pl.when(inside(da, db))
        def _(da=da, db=db):
            pl.semaphore_signal(barrier, inc=1, device_id=(row, place(da, db)), device_id_type=MESH)

    peers = sum(inside(da, db).astype(jnp.int32) for da, db in sides)
    pl.semaphore_wait(barrier, peers)

    def part(t):
        return pl.ds(pl.multiple_of(t * rows, rows), rows)

    def copy(source, block, t, side):
        da, db = sides[side]
        return pltpu.make_async_remote_copy(
            src_ref=source,
            dst_ref=full_ref.at[block, part(t)],
            send_sem=send_sem.at[side, block, t],
            recv_sem=recv_sem.at[block, t],
            device_id=(row, place(da, db)),
            device_id_type=MESH,
        )

    def keep(t):
        return pltpu.make_async_copy(own_ref.at[part(t)], full_ref.at[col, part(t)], local_sem.at[t])

    def targets(da, db, t):
        late = t >= first
        early = t < first
        chosen = []
        for side, (sa, sb) in enumerate(sides):
            if da == 0 and db == 0:
                use = inside(sa, sb)
            elif sa != 0:
                if da * sa > 0:
                    continue
                if da == 0:
                    use = inside(sa, sb) & late
                elif db == 0:
                    use = inside(sa, sb)
                else:
                    use = inside(sa, sb) & late
            else:
                if db * sb > 0:
                    continue
                if db == 0:
                    use = inside(sa, sb) & early
                elif da == 0:
                    use = inside(sa, sb)
                else:
                    use = inside(sa, sb) & early
            chosen.append((side, use))
        return chosen

    @pl.loop(0, tiles)
    def _(t):
        for side, use in targets(0, 0, t):

            @pl.when(use)
            def _(side=side):
                copy(own_ref.at[part(t)], col, t, side).start()

        keep(t).start()

    offsets = sorted(
        (
            (da, db)
            for da in range(1 - outer, outer)
            for db in range(1 - inner, inner)
            if (da, db) != (0, 0)
        ),
        key=lambda o: (abs(o[0]) + abs(o[1]), o),
    )
    far = outer + inner - 2
    for distance in range(1, far + 1):
        ring = [o for o in offsets if abs(o[0]) + abs(o[1]) == distance]

        @pl.loop(0, tiles)
        def _(t, ring=ring):
            for da, db in ring:

                @pl.when(inside(da, db))
                def _(da=da, db=db):
                    block = place(da, db)
                    landed = full_ref.at[block, part(t)]
                    copy(landed, block, t, 0).wait_recv()
                    for side, use in targets(da, db, t):

                        @pl.when(use)
                        def _(side=side):
                            copy(landed, block, t, side).start()

    @pl.loop(0, tiles)
    def _(t):
        keep(t).wait()
        for side, use in targets(0, 0, t):

            @pl.when(use)
            def _(side=side):
                copy(own_ref.at[part(t)], col, t, side).wait_send()

        for da, db in offsets:

            @pl.when(inside(da, db))
            def _(da=da, db=db):
                block = place(da, db)
                for side, use in targets(da, db, t):

                    @pl.when(use)
                    def _(side=side):
                        copy(full_ref.at[block, part(t)], block, t, side).wait_send()


def gather_columns(own, outer, inner, tiles):
    blocks = outer * inner
    rows = own.shape[0] // tiles
    first = tiles - max(1, round(tiles / 6))
    return pl.pallas_call(
        functools.partial(gather_kernel, outer, inner, tiles, first, rows),
        out_shape=jax.ShapeDtypeStruct((blocks,) + own.shape, own.dtype),
        in_specs=[pl.BlockSpec(memory_space=pl.ANY)],
        out_specs=pl.BlockSpec(memory_space=pl.ANY),
        scratch_shapes=[
            pltpu.SemaphoreType.DMA((4, blocks, tiles)),
            pltpu.SemaphoreType.DMA((blocks, tiles)),
            pltpu.SemaphoreType.DMA((tiles,)),
        ],
        compiler_params=pltpu.CompilerParams(collective_id=0, has_side_effects=True),
        cost_estimate=pl.CostEstimate(flops=0, bytes_accessed=700_000_000, transcendentals=0),
    )(own)


def update_kernel(blocks, fold, full_ref, solved_ref, mine_ref, rhs_ref, out_ref, high_ref, low_ref):
    step = pl.program_id(0)
    width = full_ref.shape[2] // fold
    piece = width // PANELS
    rows = full_ref.shape[1]

    @pl.when(step == 0)
    def _():
        for c in range(blocks):
            for p in range(PANELS):
                x = solved_ref[p * PANEL + c * piece : p * PANEL + (c + 1) * piece, :]
                high = x.astype(jnp.bfloat16)
                at = c * width + p * piece
                high_ref[at : at + piece, :] = high
                low_ref[at : at + piece, :] = (x - high.astype(jnp.float32)).astype(jnp.bfloat16)
        out_ref[...] = mine_ref[...]

    @pl.when(step > 0)
    def _():
        halves = []
        for h in range(fold):
            halves.append(
                jnp.concatenate(
                    [full_ref[c, :, h * width : (h + 1) * width] for c in range(blocks)], axis=1
                )
            )
        left = jnp.concatenate(halves, axis=0)
        high = left.astype(jnp.bfloat16)
        low = (left - high.astype(jnp.float32)).astype(jnp.bfloat16)
        dot = functools.partial(jnp.dot, preferred_element_type=jnp.float32)
        total = dot(high, low_ref[...]) + dot(low, high_ref[...])
        total = total + dot(high, high_ref[...])
        out_ref[...] = rhs_ref[...] - total


def update_rows(full, solved, mine, rhs, fold, tiles):
    blocks, packed, lanes = full.shape
    tile = mine.shape[0]
    columns = rhs.shape[1]
    rows = packed // tiles
    window = solved.shape[0]
    return pl.pallas_call(
        functools.partial(update_kernel, blocks, fold),
        grid=(tiles + 1,),
        out_shape=jax.ShapeDtypeStruct(rhs.shape, rhs.dtype),
        in_specs=[
            pl.BlockSpec((blocks, rows, lanes), lambda i: (0, jnp.maximum(i - 1, 0), 0)),
            pl.BlockSpec((window, columns), lambda i: (0, 0)),
            pl.BlockSpec((tile, columns), lambda i: (0, 0)),
            pl.BlockSpec((tile, columns), lambda i: (i, 0)),
        ],
        out_specs=pl.BlockSpec((tile, columns), lambda i: (i, 0)),
        scratch_shapes=[
            pltpu.VMEM((window, columns), jnp.bfloat16),
            pltpu.VMEM((window, columns), jnp.bfloat16),
        ],
        compiler_params=pltpu.CompilerParams(vmem_limit_bytes=60 * 1024 * 1024),
    )(full, solved, mine, rhs)


def invert_lower(blocks):
    size = blocks.shape[-1]
    r = lax.broadcasted_iota(jnp.int32, (size, size), 0)
    c = lax.broadcasted_iota(jnp.int32, (size, size), 1)
    multiply = functools.partial(
        jnp.einsum, "bij,bjk->bik", precision=HIGHEST, preferred_element_type=jnp.float32
    )
    inverse = jnp.where(r == c, 1.0 / jnp.where(r == c, blocks, 1.0), 0.0)
    width = 1
    while width < size:
        off = (r // (2 * width) == c // (2 * width)) & (r // width != c // width)
        inner = jnp.where(off, blocks, 0.0)
        inverse = inverse - multiply(multiply(inverse, inner), inverse)
        width *= 2
    return inverse


def local(rhs_tile, factor, inner):
    row_count = lax.axis_size("row")
    col_count = lax.axis_size("col")
    row_piece = PANEL // row_count
    col_piece = PANEL // col_count
    my_row = lax.axis_index("row")
    window = PANELS * row_piece
    rows, width = factor.shape
    columns = rhs_tile.shape[1]
    tiles = (rows - window) // window
    fold = 128 // math.gcd(width, 128)

    own = factor[window:].reshape(tiles, fold, window // fold, width)
    own = own.transpose(0, 2, 1, 3).reshape(tiles * window // fold, fold * width)

    strip = lax.all_gather(factor[:window], "col", axis=0)
    lower = lax.all_gather(strip, "row", axis=0)
    stacked = lax.all_gather(rhs_tile[:window], "row", axis=0)
    full = gather_columns(own, col_count // inner, inner, tiles)

    total = PANELS * PANEL
    lower = lower.reshape(row_count, col_count, PANELS, row_piece, PANELS, col_piece)
    lower = lower.transpose(2, 0, 3, 4, 1, 5).reshape(total, total)
    stacked = stacked.reshape(row_count, PANELS, row_piece, columns)
    stacked = stacked.transpose(1, 0, 2, 3).reshape(total, columns)
    diagonal = jnp.stack(
        [lower[p * PANEL : (p + 1) * PANEL, p * PANEL : (p + 1) * PANEL] for p in range(PANELS)]
    )
    inverse = invert_lower(diagonal)
    multiply = functools.partial(jnp.dot, precision=HIGHEST, preferred_element_type=jnp.float32)
    solved = multiply(inverse[0], stacked[:PANEL])
    for p in range(1, PANELS):
        at = p * PANEL
        rest = stacked[at : at + PANEL] - multiply(lower[at : at + PANEL, :at], solved)
        solved = jnp.concatenate([solved, multiply(inverse[p], rest)], axis=0)
    mine = lax.dynamic_slice_in_dim(
        solved.reshape(PANELS, PANEL, columns), my_row * row_piece, row_piece, 1
    ).reshape(window, columns)
    return update_rows(full, solved, mine, rhs_tile, fold, tiles)


def inner_size(mesh):
    count = mesh.shape["col"]
    try:
        where = [tuple(d.coords) for d in mesh.devices.reshape(-1, count)[0]]
        inner = 1
        while inner < count and sum(p != q for p, q in zip(where[inner], where[0])) == 1 and (
            inner == 1 or [p != q for p, q in zip(where[inner], where[0])]
            == [p != q for p, q in zip(where[1], where[0])]
        ):
            inner += 1
        if count % inner == 0:
            return inner
    except Exception:
        pass
    return 2 if count % 2 == 0 else 1


def solution(mesh):
    specs = P("row", "col")
    body = functools.partial(local, inner=inner_size(mesh))
    return jax.shard_map(body, mesh=mesh, in_specs=(specs, specs), out_specs=specs, check_vma=False)
```

time: 718 us -> 627 us (0.87)
  Pallas kernels: 0 us -> 323 us
  other arithmetic: 140 us -> 6.36 us
  waiting for transfers between devices: 170 us -> 53.3 us
  blocking collectives: 100 us -> 0 us
  matrix products: 163 us -> 129 us
  local copies, waits for them, and re-layouts: 120 us -> 97.1 us
    pallas_call x0 -> x2, Pallas kernels: none -> 323 us  [the longest x1 261 us: gather_columns(): pl.pallas_call(functools.partial(gather_kernel, outer, inner, tiles, firs...]
    another operation x10 -> x0, other arithmetic: 125 us -> none  [local(): solved = jax.scipy.linalg.solve_triangular(diagonal, stacked, lower=True)]
    all_gather x9 -> x3, waiting for transfers between devices: 170 us -> 53.2 us  [the longest x1 53.2 us: local(): strip = lax.all_gather(factor[:window], 'col', axis=0)]
    all_gather x3 -> x0, blocking collectives: 100 us -> none  [local(): lax.all_gather(factor[start_row:end_row, first_col:first_col + col_piece]...]
    reshape x0 -> x6, local copies, waits for them, and re-layouts: none -> 57.1 us  [the longest x1 14.7 us: local(): lower.reshape(row_count, col_count, PANELS, row_piece, PANELS, col_piece)]
    another operation x21 -> x0, matrix products: 39.1 us -> none  [local(): solved = jax.scipy.linalg.solve_triangular(diagonal, stacked, lower=True)]
    another operation x70 -> x0, local copies, waits for them, and re-layouts: 36 us -> none  [local(): solved = jax.scipy.linalg.solve_triangular(diagonal, stacked, lower=True)]
    unnamed x27, local copies, waits for them, and re-layouts: 30.6 us -> 5.09 us
  transfers between devices with their start and end apart: 9 -> 3, of which waited for: 3 -> 1; matrix products, arithmetic and copies ran while one was open for 47% -> 8% of each run, Pallas kernels for 0% -> 42%
where the time goes in v1:
time: 627 us; the launch traced here: 623 us
  Pallas kernels  323 us (52%)
  matrix products  129 us (21%)
  local copies, waits for them, and re-layouts  97.1 us (15%)
  waiting for transfers between devices  53.3 us (9%)
  between operations  13.8 us (2%)
  other arithmetic  6.36 us (1%)
    pallas_call x1, Pallas kernels, gather_columns(): pl.pallas_call(functools.partial(gather_kernel, outer, inner, tiles, firs...  261 us
    dot_general x18, matrix products, invert_lower(): inverse = inverse - multiply(multiply(inverse, inner), inverse)  101 us
    pallas_call x1, Pallas kernels, update_rows(): pl.pallas_call(functools.partial(update_kernel, blocks, fold), grid=(tile...  62.1 us
    all_gather x1, waiting for transfers between devices, local(): strip = lax.all_gather(factor[:window], 'col', axis=0)  53.2 us
    transpose x1, local copies, waits for them, and re-layouts, local(): lower = lower.transpose(2, 0, 3, 4, 1, 5).reshape(total, total)  15.7 us
    dot_general x2, matrix products, local(): rest = stacked[at:at + PANEL] - multiply(lower[at:at + PANEL, :at], solved)  15.2 us
    reshape x1, local copies, waits for them, and re-layouts, local(): lower.reshape(row_count, col_count, PANELS, row_piece, PANELS, col_piece)  14.7 us
    reshape x2, local copies, waits for them, and re-layouts, local(): own = factor[window:].reshape(tiles, fold, window // fold, width)  13.3 us
  transfers between devices with their start and end apart: 3, of which 1 were waited for; matrix products, arithmetic and copies ran while one was open for 8% of the time, Pallas kernels for 42%

profile of v1, /device:TPU:0, one launch (start us, length us, event | category | flops | bytes accessed | tf_op | source)
XLA Modules:
  0.0 622.6 jit_solution(9826327635001669039)
XLA Ops:
  11.2 53.2 %all-gather.7.cloned.1.call-done = f32[3072,192]{0,1:T(8,128)} async-done(((f32[384,192]{0,1:T(8,128)}), f32[3072,192]{0,1:T(8,128)}) %all-gather.7.cloned.1.call-update) | async-done | bytes 2359312 | tf_op jit(solution)/shard_map/all_gather | solution.py:254
  74.0 8.9 %copy.16 = f32[11,2,192,192]{3,1,2,0:T(2,128)} copy(f32[11,2,192,192]{2,1,0,3:T(2,128)} %reshape.25) | data formatting | bytes 6488064 | tf_op jit(solution)/shard_map/reshape | solution.py:251
  83.0 6.1 reshape.26.own_ref
  89.1 260.6 %shard_map.28.full_ref = f32[8,2112,384]{2,1,0:T(8,128)} custom-call(f32[2112,384]{1,0:T(8,128)} %reshape.26.own_ref), custom_call_target="tpu_custom_call" | custom-call | bytes 700000000 | tf_op jit(solution)/shard_map/pallas_call | solution.py:147
  355.7 10.3 %copy.22 = f32[4,3,128,1152]{2,0,3,1:T(4,128)} copy(f32[4,3,128,1152]{3,2,1,0:T(8,128)} %bitcast.121) | data formatting | bytes 14155776 | tf_op jit(solution)/shard_map/reshape | solution.py:262
  371.0 14.7 %reshape.27 = f32[4,8,3,128,3,64]{3,2,5,4,1,0:T(4,128)} reshape(f32[32,384,192]{1,2,0:T(8,128)} %all-gather.9.cloned.1.call-done) | data formatting | bytes 18874368 | tf_op jit(solution)/shard_map/reshape | solution.py:260
  385.7 15.7 %copy.18 = f32[3,4,128,3,8,64]{2,1,0,5,4,3:T(4,128)} copy(f32[3,4,128,3,8,64]{2,0,5,3,4,1:T(4,128)} %bitcast.113) | data formatting | bytes 18874368 | tf_op jit(solution)/shard_map/transpose | solution.py:261
  401.4 12.6 %reshape.28 = f32[1536,1536]{0,1:T(8,128)} reshape(f32[3,4,128,3,8,64]{2,1,0,5,4,3:T(4,128)} %copy.18) | data formatting | bytes 18874368 | tf_op jit(solution)/shard_map/reshape | solution.py:261
  419.5 7.0 %fusion.27 = f32[3,512,512]{2,1,0:T(8,128)S(1)} fusion(pred[512,512]{1,0:T(8,128)(4,1)} %get-tuple-element.19, pred[512,512]{1,0:T(8,128)(4,1)} %iota_compare_fusion.1, f32[1,512,512]{2,1,0:T(8,128)S(1)} %bitcast.103, f32[1,512,512]{2,1,0:T(8,128)S(1)} %bitcast.93, f32[1,512,512]{2,1,0:T(8,128)S(1)} %bitcast.83), kind=kOutput, calls=%fused_computation.26 | convolution fusion | flops 4838129664 | bytes 6815744 | tf_op jit(solution)/shard_map/bij,bjk->bik/dot_general | solution.py:234
  426.5 5.7 convolution_subtract_fusion.8
  432.2 5.7 fusion.25
  443.2 5.8 fusion.23
  454.3 5.9 fusion.21
  465.5 5.5 fusion.19
  471.1 5.5 convolution_subtract_fusion.4
  476.6 5.5 fusion.17
  482.1 5.5 convolution_subtract_fusion.3
  487.7 5.5 fusion.15
  498.5 5.9 fusion.13
  504.4 5.3 convolution_subtract_fusion.1
  509.7 5.7 fusion.11
  525.2 5.5 fusion.10
  535.1 9.7 %fusion.7 = f32[512,1152]{0,1:T(8,128)S(1)} fusion(f32[512,1152]{1,0:T(8,128)S(1)} %fusion.58, f32[512,1152]{1,0:T(8,128)S(1)} %fusion.29, f32[144,8,4,128]{3,2,1,0:T(4,128)S(1)} %bitcast.119, f32[1536,1536]{0,1:T(8,128)} %reshape.28), kind=kOutput, calls=%fused_computation.6 | convolution fusion | flops 7249526784 | bytes 11534336 | tf_op jit(solution)/shard_map/dot_general | solution.py:272
  553.8 62.1 %shard_map.29 = f32[4608,1152]{1,0:T(8,128)} custom-call(f32[8,2112,384]{2,1,0:T(8,128)} %shard_map.28.full_ref, f32[1536,1152]{1,0:T(8,128)} %copy-done, f32[384,1152]{1,0:T(8,128)} %bitcast.122, f32[4608,1152]{1,0:T(8,128)} %rhs_ref.1), custom_call_target="tpu_custom_call" | custom-call | tf_op jit(solution)/shard_map/pallas_call | solution.py:203
  (70 shorter events, 74.9 us)
Async XLA Ops:
  6.5 57.9 %all-gather.7.cloned.1.call-start = ((), (), s32[]{:S(2)}) async-start(), calls=%async_computation | async-start | bytes 2654208 | tf_op jit(solution)/shard_map/all_gather | solution.py:254
  8.3 347.4 %all-gather.11.cloned.1.call-start = ((), (), s32[]{:S(2)}) async-start(), calls=%async_computation.2 | async-start | bytes 8847360 | tf_op jit(solution)/shard_map/all_gather | solution.py:256
  11.2 359.8 %all-gather.9.cloned.1.call-start = ((), (), s32[]{:S(2)}) async-start(), calls=%async_computation.1 | async-start | bytes 11796480 | tf_op jit(solution)/shard_map/all_gather | solution.py:255
  67.7 1.9 slice-start
  419.5 7.0 %copy-start.11 = (pred[512,512]{1,0:T(8,128)(4,1)S(1)}, pred[512,512]{1,0:T(8,128)(4,1)}, u32[]{:S(2)}) copy-start(pred[512,512]{1,0:T(8,128)(4,1)} %iota_compare_fusion.1) | copy-start | bytes 786436
  426.5 5.7 copy-start.8
  437.9 5.3 copy-start.6
  449.0 5.3 copy-start.4
  460.2 5.3 copy-start.10
  471.1 5.5 copy-start.9
  482.1 5.5 copy-start.7
  493.2 5.3 copy-start.5
  515.4 5.3 copy-start.1
  520.7 4.4 copy-start.3
  530.6 4.4 copy-start.2
  549.7 2.8 copy-start
Sparse Core Ops, SparseCore 0:
  9.5 54.9 all-gather.6
  66.0 49.1 all-gather.10
  116.8 64.2 all-gather.8

commit v2 on v1

v2 whole, which is shorter than its diff:
```python
import functools
import math

import jax
import jax.numpy as jnp
from jax import lax
from jax.experimental import pallas as pl
from jax.experimental.pallas import tpu as pltpu
from jax.sharding import PartitionSpec as P

PANEL = 512
PANELS = 3
HIGHEST = lax.Precision.HIGHEST
MESH = pl.DeviceIdType.MESH


def gather_kernel(
    outer, inner, peers, tiles, first, rows,
    own_ref, full_ref, window_ref, send_sem, recv_sem, local_sem, push_sem, pull_sem, stay_sem,
):
    row = lax.axis_index("row")
    col = lax.axis_index("col")
    a, b = lax.div(col, inner), lax.rem(col, inner)
    sides = ((1, 0), (-1, 0), (0, 1), (0, -1))

    def inside(da, db):
        return (a + da >= 0) & (a + da < outer) & (b + db >= 0) & (b + db < inner)

    def place(da, db):
        return (a + da) * inner + b + db

    barrier = pltpu.get_barrier_semaphore()
    for da, db in sides:

        @pl.when(inside(da, db))
        def _(da=da, db=db):
            pl.semaphore_signal(barrier, inc=1, device_id=(row, place(da, db)), device_id_type=MESH)

    for k in range(1, peers):
        pl.semaphore_signal(
            barrier, inc=1, device_id=(lax.rem(row + k, peers), col), device_id_type=MESH
        )
    near = sum(inside(da, db).astype(jnp.int32) for da, db in sides)
    pl.semaphore_wait(barrier, near + peers - 1)

    def part(t):
        return pl.ds(pl.multiple_of(t * rows, rows), rows)

    def copy(source, block, t, side):
        da, db = sides[side]
        return pltpu.make_async_remote_copy(
            src_ref=source,
            dst_ref=full_ref.at[block, part(t)],
            send_sem=send_sem.at[side, block, t],
            recv_sem=recv_sem.at[block, t],
            device_id=(row, place(da, db)),
            device_id_type=MESH,
        )

    def keep(t):
        return pltpu.make_async_copy(own_ref.at[part(t)], full_ref.at[col, part(t)], local_sem.at[t])

    def targets(da, db, t):
        late = t >= first
        early = t < first
        chosen = []
        for side, (sa, sb) in enumerate(sides):
            if da == 0 and db == 0:
                use = inside(sa, sb)
            elif sa != 0:
                if da * sa > 0:
                    continue
                if da == 0:
                    use = inside(sa, sb) & late
                elif db == 0:
                    use = inside(sa, sb)
                else:
                    use = inside(sa, sb) & late
            else:
                if db * sb > 0:
                    continue
                if db == 0:
                    use = inside(sa, sb) & early
                elif da == 0:
                    use = inside(sa, sb)
                else:
                    use = inside(sa, sb) & early
            chosen.append((side, use))
        return chosen

    def launch(t):
        for side, use in targets(0, 0, t):

            @pl.when(use)
            def _(side=side):
                copy(own_ref.at[part(t)], col, t, side).start()

        keep(t).start()

    def push(k, c, sender):
        return pltpu.make_async_remote_copy(
            src_ref=full_ref.at[c, part(0)],
            dst_ref=window_ref.at[sender, c],
            send_sem=push_sem.at[k, c],
            recv_sem=pull_sem.at[sender, c],
            device_id=(lax.rem(row + k, peers), col),
            device_id_type=MESH,
        )

    def stay(c):
        return pltpu.make_async_copy(full_ref.at[c, part(0)], window_ref.at[row, c], stay_sem.at[c])

    lead = min(3, tiles)
    pl.loop(0, lead)(launch)

    offsets = sorted(
        (
            (da, db)
            for da in range(1 - outer, outer)
            for db in range(1 - inner, inner)
            if (da, db) != (0, 0)
        ),
        key=lambda o: (abs(o[0]) + abs(o[1]), o),
    )
    far = outer + inner - 2
    rings = [[o for o in offsets if abs(o[0]) + abs(o[1]) == d] for d in range(1, far + 1)]

    def pass_on(t, ring):
        for da, db in ring:

            @pl.when(inside(da, db))
            def _(da=da, db=db):
                block = place(da, db)
                landed = full_ref.at[block, part(t)]
                copy(landed, block, t, 0).wait_recv()
                for side, use in targets(da, db, t):

                    @pl.when(use)
                    def _(side=side):
                        copy(landed, block, t, side).start()

    for ring in rings:
        pl.loop(0, 1)(functools.partial(pass_on, ring=ring))
    pl.loop(lead, tiles)(launch)
    keep(0).wait()

    @pl.loop(0, outer * inner)
    def _(c):
        for k in range(1, peers):
            push(k, c, row).start()
        stay(c).start()

    for ring in rings:
        pl.loop(1, tiles)(functools.partial(pass_on, ring=ring))

    @pl.loop(0, outer * inner)
    def _(c):
        stay(c).wait()
        for k in range(1, peers):
            push(k, c, row).wait_send()
            push(k, c, lax.rem(row + peers - k, peers)).wait_recv()

    @pl.loop(1, tiles)
    def _(t):
        keep(t).wait()

    @pl.loop(0, tiles)
    def _(t):
        for side, use in targets(0, 0, t):

            @pl.when(use)
            def _(side=side):
                copy(own_ref.at[part(t)], col, t, side).wait_send()

        for da, db in offsets:

            @pl.when(inside(da, db))
            def _(da=da, db=db):
                block = place(da, db)
                for side, use in targets(da, db, t):

                    @pl.when(use)
                    def _(side=side):
                        copy(full_ref.at[block, part(t)], block, t, side).wait_send()


def gather_columns(own, outer, inner, peers, tiles):
    blocks = outer * inner
    rows = own.shape[0] // tiles
    first = tiles - max(1, round(tiles / 6))
    return pl.pallas_call(
        functools.partial(gather_kernel, outer, inner, peers, tiles, first, rows),
        out_shape=[
            jax.ShapeDtypeStruct((blocks,) + own.shape, own.dtype),
            jax.ShapeDtypeStruct((peers, blocks, rows, own.shape[1]), own.dtype),
        ],
        in_specs=[pl.BlockSpec(memory_space=pl.ANY)],
        out_specs=[pl.BlockSpec(memory_space=pl.ANY)] * 2,
        scratch_shapes=[
            pltpu.SemaphoreType.DMA((4, blocks, tiles)),
            pltpu.SemaphoreType.DMA((blocks, tiles)),
            pltpu.SemaphoreType.DMA((tiles,)),
            pltpu.SemaphoreType.DMA((peers, blocks)),
            pltpu.SemaphoreType.DMA((peers, blocks)),
            pltpu.SemaphoreType.DMA((blocks,)),
        ],
        compiler_params=pltpu.CompilerParams(collective_id=0, has_side_effects=True),
        cost_estimate=pl.CostEstimate(flops=0, bytes_accessed=700_000_000, transcendentals=0),
    )(own)


def invert_lower(block):
    size = block.shape[-1]
    r = lax.broadcasted_iota(jnp.int32, (size, size), 0)
    c = lax.broadcasted_iota(jnp.int32, (size, size), 1)
    inverse = jnp.where(r == c, 1.0 / jnp.where(r == c, block, 1.0), 0.0)
    shift = 0
    while (1 << shift) < size:
        off = ((r >> (shift + 1)) == (c >> (shift + 1))) & ((r >> shift) != (c >> shift))
        inner = jnp.where(off, block, 0.0)
        inverse = inverse - exact(exact(inverse, inner), inverse)
        shift += 1
    return inverse


def exact(x, y):
    return jnp.dot(x, y, precision=HIGHEST, preferred_element_type=jnp.float32)


def solve(window_ref, strip_ref, strip_sem, lower_ref, x_ref, inverse_ref):
    peers, blocks, rows, lanes = window_ref.shape
    own = x_ref.shape[0] // peers
    fold = own // rows
    width = lanes // fold
    piece = width // PANELS
    row_piece = PANEL // peers

    def fetch(r):
        return pltpu.make_async_copy(window_ref.at[r], strip_ref, strip_sem.at[r % 2])

    for r in range(peers):
        fetch(r).start()
        fetch(r).wait()
        for h in range(fold):
            at = r * own + h * rows
            for p in range(PANELS):
                left = h * width + p * piece
                lower_ref[p, at : at + rows, :] = jnp.concatenate(
                    [strip_ref[c, :, left : left + piece] for c in range(blocks)], axis=1
                )
    groups = [(p, r) for p in range(PANELS) for r in range(peers)]

    @pl.loop(0, PANELS)
    def _(p):
        for r in range(peers):
            at = pl.multiple_of(r * own + p * row_piece, row_piece)
            block = lower_ref[p, pl.ds(at, row_piece), r * row_piece : (r + 1) * row_piece]
            inverse_ref[p * peers + r] = invert_lower(block)

    for p, r in groups:
        at = r * own + p * row_piece
        here = p * PANEL + r * row_piece
        rest = x_ref[here : here + row_piece, :]
        for q in range(p):
            rest = rest - exact(
                lower_ref[q, at : at + row_piece, :], x_ref[q * PANEL : (q + 1) * PANEL, :]
            )
        if r > 0:
            rest = rest - exact(
                lower_ref[p, at : at + row_piece, : r * row_piece], x_ref[p * PANEL : here, :]
            )
        x_ref[here : here + row_piece, :] = exact(inverse_ref[p * peers + r], rest)


def update_kernel(
    full_ref, window_ref, stacked_ref, rhs_ref, out_ref, high_ref, low_ref, lower_ref, x_ref, inverse_ref, load_sem,
    strip_ref, strip_sem,
):
    step = pl.program_id(0)
    peers, blocks, rows, lanes = window_ref.shape
    tile = out_ref.shape[0]
    fold = tile // rows
    width = lanes // fold
    piece = width // PANELS
    row_piece = PANEL // peers

    @pl.when(step == 0)
    def _():
        copies = [
            pltpu.make_async_copy(
                stacked_ref.at[r, pl.ds(p * row_piece, row_piece)],
                x_ref.at[pl.ds(p * PANEL + r * row_piece, row_piece)],
                load_sem.at[p, r],
            )
            for p in range(PANELS)
            for r in range(peers)
        ]
        for one in copies:
            one.start()
        for one in copies:
            one.wait()
        solve(window_ref, strip_ref, strip_sem, lower_ref, x_ref, inverse_ref)
        for c in range(blocks):
            for p in range(PANELS):
                x = x_ref[p * PANEL + c * piece : p * PANEL + (c + 1) * piece, :]
                high = x.astype(jnp.bfloat16)
                at = c * width + p * piece
                high_ref[at : at + piece, :] = high
                low_ref[at : at + piece, :] = (x - high.astype(jnp.float32)).astype(jnp.bfloat16)
        mine = lax.axis_index("row") * row_piece
        for p in range(PANELS):
            at = pl.multiple_of(p * PANEL + mine, row_piece)
            out_ref[p * row_piece : (p + 1) * row_piece, :] = x_ref[pl.ds(at, row_piece), :]

    @pl.when(step > 0)
    def _():
        halves = []
        for h in range(fold):
            halves.append(
                jnp.concatenate(
                    [full_ref[c, :, h * width : (h + 1) * width] for c in range(blocks)], axis=1
                )
            )
        left = jnp.concatenate(halves, axis=0)
        high = left.astype(jnp.bfloat16)
        low = (left - high.astype(jnp.float32)).astype(jnp.bfloat16)
        dot = functools.partial(jnp.dot, preferred_element_type=jnp.float32)
        columns = out_ref.shape[1]
        part = columns // 3 if columns % 384 == 0 else columns

        @pl.loop(0, columns // part)
        def _(n):
            at = pl.ds(pl.multiple_of(n * part, part), part)
            total = dot(high, low_ref[:, at]) + dot(low, high_ref[:, at])
            total = total + dot(high, high_ref[:, at])
            out_ref[:, at] = rhs_ref[:, at] - total


def update_rows(full, window, stacked, rhs, tiles):
    blocks, packed, lanes = full.shape
    peers, _, rows, _ = window.shape
    tile = stacked.shape[1]
    columns = rhs.shape[1]
    total = peers * tile
    row_piece = PANEL // peers
    return pl.pallas_call(
        update_kernel,
        grid=(tiles,),
        out_shape=jax.ShapeDtypeStruct(rhs.shape, rhs.dtype),
        in_specs=[
            pl.BlockSpec((blocks, rows, lanes), lambda i: (0, i, 0)),
            pl.BlockSpec(memory_space=pl.ANY),
            pl.BlockSpec(memory_space=pl.ANY),
            pl.BlockSpec((tile, columns), lambda i: (i, 0)),
        ],
        out_specs=pl.BlockSpec((tile, columns), lambda i: (i, 0)),
        scratch_shapes=[
            pltpu.VMEM((total, columns), jnp.bfloat16),
            pltpu.VMEM((total, columns), jnp.bfloat16),
            pltpu.VMEM((PANELS, total, PANEL), jnp.float32),
            pltpu.VMEM((total, columns), jnp.float32),
            pltpu.VMEM((PANELS * peers, row_piece, row_piece), jnp.float32),
            pltpu.SemaphoreType.DMA((PANELS, peers)),
            pltpu.VMEM((blocks, rows, lanes), jnp.float32),
            pltpu.SemaphoreType.DMA((2,)),
        ],
        compiler_params=pltpu.CompilerParams(vmem_limit_bytes=67_043_328),
    )(full, window, stacked, rhs)


def local(rhs_tile, factor, inner):
    row_count = lax.axis_size("row")
    col_count = lax.axis_size("col")
    window = PANELS * (PANEL // row_count)
    rows, width = factor.shape
    tiles = rows // window
    fold = 128 // math.gcd(width, 128)

    own = factor.reshape(tiles, fold, window // fold, width)
    own = own.transpose(0, 2, 1, 3).reshape(rows // fold, fold * width)
    stacked = lax.all_gather(rhs_tile[:window], "row", axis=0)
    full, strips = gather_columns(own, col_count // inner, inner, row_count, tiles)
    return update_rows(full, strips, stacked, rhs_tile, tiles)


def inner_size(mesh):
    count = mesh.shape["col"]
    try:
        where = [tuple(d.coords) for d in mesh.devices.reshape(-1, count)[0]]
        inner = 1
        while inner < count and sum(p != q for p, q in zip(where[inner], where[0])) == 1 and (
            inner == 1 or [p != q for p, q in zip(where[inner], where[0])]
            == [p != q for p, q in zip(where[1], where[0])]
        ):
            inner += 1
        if count % inner == 0:
            return inner
    except Exception:
        pass
    return 2 if count % 2 == 0 else 1


def solution(mesh):
    specs = P("row", "col")
    body = functools.partial(local, inner=inner_size(mesh))
    return jax.shard_map(body, mesh=mesh, in_specs=(specs, specs), out_specs=specs, check_vma=False)
```

time: 627 us -> 511 us (0.81)
  Pallas kernels: 323 us -> 466 us
  matrix products: 129 us -> 0 us
  local copies, waits for them, and re-layouts: 97.1 us -> 24.8 us
  waiting for transfers between devices: 53.3 us -> 0.04 us
  other arithmetic: 6.36 us -> 0 us
    pallas_call x2, Pallas kernels: 323 us -> 466 us  [the longest x1 295 us: gather_columns(): pl.pallas_call(functools.partial(gather_kernel, outer, inner, peers, tile...]
    dot_general x23 -> x0, matrix products: 129 us -> none  [the longest x18 101 us: invert_lower(): inverse = inverse - multiply(multiply(inverse, inner), inverse)]
    all_gather x2 -> x0, waiting for transfers between devices: 53.2 us -> none  [the longest x1 53.2 us: local(): strip = lax.all_gather(factor[:window], 'col', axis=0)]
    reshape x6 -> x3, local copies, waits for them, and re-layouts: 57.1 us -> 21.8 us  [the longest x2 15.3 us: local(): own = factor.reshape(tiles, fold, window // fold, width)]
    transpose x1 -> x0, local copies, waits for them, and re-layouts: 15.7 us -> none  [local(): lower = lower.transpose(2, 0, 3, 4, 1, 5).reshape(total, total)]
    slice x5 -> x0, local copies, waits for them, and re-layouts: 11.9 us -> none  [the longest x1 5.02 us: local(): rest = stacked[at:at + PANEL] - multiply(lower[at:at + PANEL, :at], solved)]
  transfers between devices with their start and end apart: 3 -> 1, of which waited for: 1 -> 0; matrix products, arithmetic and copies ran while one was open for 8% -> 4% of each run, Pallas kernels for 42% -> 58%
where the time goes in v2:
time: 511 us; the launch traced here: 504 us
  Pallas kernels  466 us (91%)
  local copies, waits for them, and re-layouts  24.8 us (5%)
  between operations  13.8 us (3%)
    pallas_call x1, Pallas kernels, gather_columns(): pl.pallas_call(functools.partial(gather_kernel, outer, inner, peers, tile...  295 us
    pallas_call x1, Pallas kernels, update_rows(): pl.pallas_call(update_kernel, grid=(tiles,), out_shape=jax.ShapeDtypeStru...  171 us
    reshape x2, local copies, waits for them, and re-layouts, local(): own = factor.reshape(tiles, fold, window // fold, width)  15.3 us
  transfers between devices with their start and end apart: 1, of which 0 were waited for; matrix products, arithmetic and copies ran while one was open for 4% of the time, Pallas kernels for 58%

profile of v2, /device:TPU:0, one launch (start us, length us, event | category | flops | bytes accessed | tf_op | source)
XLA Modules:
  0.0 504.5 jit_solution(4679773660262914821)
XLA Ops:
  6.5 0.0 copy-start
  6.5 0.0 all-gather.3.cloned.1.call-start
  6.5 3.0 slice.3
  9.5 0.0 all-gather.3.cloned.1.call-update
  9.5 0.0 copy-done
  9.5 5.5 %reshape.6 = f32[12,2,192,192]{2,1,0,3:T(2,128)} reshape(f32[4608,192]{0,1:T(8,128)S(1)} %copy-done) | data formatting | bytes 7077888 | tf_op jit(solution)/shard_map/reshape | solution.py:379
  15.0 9.8 %copy.3 = f32[12,2,192,192]{3,1,2,0:T(2,128)} copy(f32[12,2,192,192]{2,1,0,3:T(2,128)} %reshape.6) | data formatting | bytes 7077888 | tf_op jit(solution)/shard_map/reshape | solution.py:379
  24.8 6.6 %reshape.7.own_ref = f32[2304,384]{1,0:T(8,128)} reshape(f32[12,192,2,192]{3,2,1,0:T(2,128)} %bitcast.4) | data formatting | bytes 7077888 | tf_op jit(solution)/shard_map/reshape | solution.py:380
  31.4 295.1 %shard_map.28 = (f32[8,2304,384]{2,1,0:T(8,128)}, f32[4,8,192,384]{3,2,1,0:T(8,128)}) custom-call(f32[2304,384]{1,0:T(8,128)} %reshape.7.own_ref), custom_call_target="tpu_custom_call" | custom-call | bytes 700000000 | tf_op jit(solution)/shard_map/pallas_call | solution.py:191
  326.4 0.0 all-gather.3.cloned.1.call-done
  326.5 170.8 %shard_map.29 = f32[4608,1152]{1,0:T(8,128)} custom-call(f32[8,2304,384]{2,1,0:T(8,128)} %get-tuple-element.7.full_ref, f32[4,8,192,384]{3,2,1,0:T(8,128)} %get-tuple-element.8.window_ref, f32[4,384,1152]{2,1,0:T(8,128)} %bitcast.5, f32[4608,1152]{1,0:T(8,128)} %rhs_ref.1), custom_call_target="tpu_custom_call" | custom-call | tf_op jit(solution)/shard_map/pallas_call | solution.py:346
Async XLA Ops:
  6.5 3.0 copy-start
  6.5 319.9 %all-gather.3.cloned.1.call-start = ((), (), s32[]{:S(2)}) async-start(), calls=%async_computation | async-start | bytes 8847360 | tf_op jit(solution)/shard_map/all_gather | solution.py:381
Sparse Core Ops, SparseCore 0:
  9.7 53.5 all-gather.2
